TPU v7x, 256 devices: a whole 4x4x8 slice. The times are simulated.
256 devices in a mesh: dp: 16 (over x, z_lo), shard: 16 (over z_hi, y, core).
Axes of the slice: x: 4, y: 4, z: 8 (z_hi: 2, z_lo: 4; z = z_hi * 4 + z_lo), core: 2. Of those that a mesh axis runs over, the one named last changes fastest.
Arguments:
- codes: int32 [16, 5, 8, 64], P('dp', None, None, 'shard'), may hold values from 0 to 262143
- lengths: int32 [16], P('dp'), may hold values from 1 to 5, 48 in all
- hidden: bfloat16 [16, 5, 8, 64, 512], P('dp', None, None, 'shard'), may hold values from -6 to 6
- embed: bfloat16 [18, 512], replicated, may hold values from -1.5 to 1.5
- conv_weight: bfloat16 [512, 27, 512], P('shard'), may hold values from -0.0546875 to 0.0546875
- gain: float32 [512], replicated, may hold values from 0.1 to 1.9
- bias: float32 [512], replicated, may hold values from -3 to 3
- cotangent: bfloat16 [16, 5, 16, 128, 128], P('dp', None, None, 'shard'), may hold values from -6 to 6
Outputs:
- decoded: bfloat16 [16, 5, 16, 128, 128], P('dp', None, None, 'shard')
- grad_hidden: bfloat16 [16, 5, 8, 64, 512], P('dp', None, None, 'shard')
- grad_conv: float32 [512, 27, 512], P('shard')
- grad_embed: float32 [18, 512], replicated
- grad_gain: float32 [512], replicated
- grad_bias: float32 [512], replicated
Inputs may be any that keep to these rules, and one draw needn't show every extreme that they name: Frames from lengths[c] on are padding; some clip has all 5 frames valid.
All inputs are finite; a program needn't handle non-finite values. No bound on the sum of `lengths` on one device may be relied on, other than what follows from the above.
Results may differ from a plain program's by a relative error of at most 0.02.
Values may be sent and summed in bfloat16 or wider, within the bound.
A program may use at most 128 MiB of HBM per device.

v0:
```python
import jax
import jax.numpy as jnp
from jax import lax
from jax.sharding import PartitionSpec as P

CODE_BITS = 18
GROUPS = 32
eps_norm = 1e-05


def forward_taps(padded, frames, height, width):
    taps = []
    for depth_tap in range(3):
        for row_tap in range(3):
            for col_tap in range(3):
                taps.append(
                    padded[
                        depth_tap : depth_tap + frames,
                        row_tap : row_tap + height,
                        col_tap : col_tap + width,
                    ]
                )
    return taps


def backward_taps(padded, frames, height, width):
    taps = []
    for depth_tap in range(3):
        for row_tap in range(3):
            for col_tap in range(3):
                taps.append(
                    padded[
                        2 - depth_tap : 2 - depth_tap + frames,
                        2 - row_tap : 2 - row_tap + height,
                        2 - col_tap : 2 - col_tap + width,
                    ]
                )
    return taps


def slab_columns(spread, frames, height, slab_width):
    padded = jnp.pad(spread, ((2, 0), (1, 1), (1, 1), (0, 0)))
    return jnp.concatenate(forward_taps(padded, frames, height, slab_width), axis=3)


def on_device(codes, lengths, hidden, embed, conv_weight, gain, bias, cotangent):
    frames = codes.shape[1]
    height = codes.shape[2]
    width = codes.shape[3]
    share = conv_weight.shape[0]
    channels = conv_weight.shape[2]
    quarter = channels // 4
    shards = lax.axis_size("shard")
    slab_width = width * shards
    positions = frames * height * width
    groups = GROUPS
    per_group = channels // groups
    frame_mask = (jnp.arange(frames) < lengths[0]).astype(jnp.float32)
    mask_cells = frame_mask[:, None, None, None]
    mask_groups = frame_mask[:, None, None, None, None]
    powers = 2 ** jnp.arange(CODE_BITS, dtype=jnp.int32)
    bits = (codes[0][..., None] // powers % 2 * 2 - 1).astype(jnp.bfloat16)
    embedded = jnp.dot(
        bits.reshape(positions, CODE_BITS), embed, preferred_element_type=jnp.float32
    ).reshape(frames, height, width, channels)
    features = ((embedded + hidden[0].astype(jnp.float32)) * mask_cells).astype(jnp.bfloat16)
    spread = lax.all_to_all(features, "shard", split_axis=3, concat_axis=2, tiled=True)
    slab_patches = slab_columns(spread, frames, height, slab_width)
    flat_share = jnp.transpose(conv_weight, (1, 0, 2)).reshape(27 * share, channels)
    part_sums = jnp.dot(
        slab_patches.reshape(-1, 27 * share), flat_share, preferred_element_type=jnp.float32
    ).reshape(frames, height, slab_width, channels)
    conv_out = lax.psum_scatter(
        part_sums.astype(jnp.bfloat16), "shard", scatter_dimension=2, tiled=True
    ).astype(jnp.float32)
    grouped = conv_out.reshape(frames, height, width, groups, per_group)
    sum_one, sum_two = lax.psum(
        (
            jnp.sum(grouped * mask_groups, axis=(0, 1, 2, 4)),
            jnp.sum(grouped * grouped * mask_groups, axis=(0, 1, 2, 4)),
        ),
        "shard",
    )
    count = lengths[0].astype(jnp.float32) * (height * width * shards * per_group)
    mean = sum_one / count
    variance = sum_two / count - mean * mean
    inv_std = lax.rsqrt(variance + eps_norm)
    gain_group = gain.reshape(groups, per_group)
    bias_group = bias.reshape(groups, per_group)
    normed = (grouped - mean[:, None]) * inv_std[:, None]
    pre = normed * gain_group + bias_group
    sigma = jax.nn.sigmoid(pre)
    activated = pre * sigma * mask_groups
    decoded = (
        activated.reshape(frames, height, width, 2, 2, quarter)
        .transpose(0, 1, 3, 2, 4, 5)
        .reshape(frames, 2 * height, 2 * width, quarter)
        .astype(jnp.bfloat16)[None]
    )
    upstream = (
        cotangent[0]
        .astype(jnp.float32)
        .reshape(frames, height, 2, width, 2, quarter)
        .transpose(0, 1, 3, 2, 4, 5)
        .reshape(frames, height, width, groups, per_group)
        * mask_groups
    )
    d_pre = upstream * sigma * (1.0 + pre * (1.0 - sigma))
    gain_term = jnp.sum(d_pre * normed, axis=(0, 1, 2)).reshape(channels)
    bias_term = jnp.sum(d_pre, axis=(0, 1, 2)).reshape(channels)
    d_norm = d_pre * gain_group
    tot_one, tot_two = lax.psum(
        (jnp.sum(d_norm, axis=(0, 1, 2, 4)), jnp.sum(d_norm * normed, axis=(0, 1, 2, 4))), "shard"
    )
    d_conv = (
        (
            inv_std[:, None]
            * (d_norm - tot_one[:, None] / count - normed * tot_two[:, None] / count)
            * mask_groups
        )
        .reshape(frames, height, width, channels)
        .astype(jnp.bfloat16)
    )
    whole_grad = lax.all_gather(d_conv, "shard", axis=2, tiled=True)
    back_share = jnp.transpose(conv_weight, (2, 1, 0)).reshape(channels, 27 * share)
    tap_images = jnp.dot(
        whole_grad.reshape(-1, channels), back_share, preferred_element_type=jnp.float32
    ).reshape(frames, height, slab_width, 27 * share)
    padded_images = jnp.pad(tap_images, ((0, 2), (1, 1), (1, 1), (0, 0)))
    input_sum = jnp.zeros((frames, height, slab_width, share), jnp.float32)
    for tap_index, shifted in enumerate(backward_taps(padded_images, frames, height, slab_width)):
        input_sum = input_sum + shifted[..., tap_index * share : (tap_index + 1) * share]
    d_features = lax.all_to_all(
        input_sum.astype(jnp.bfloat16), "shard", split_axis=2, concat_axis=3, tiled=True
    )
    clip_part = jnp.einsum(
        "pk,pc->kc",
        slab_patches.reshape(-1, 27 * share),
        whole_grad.reshape(-1, channels),
        preferred_element_type=jnp.float32,
    )
    weight_sum = clip_part.reshape(27, share, channels).transpose(1, 0, 2)
    grad_conv = lax.psum(weight_sum.astype(jnp.bfloat16), "dp").astype(jnp.float32)
    grad_hidden = d_features * mask_cells.astype(jnp.bfloat16)
    embed_term = jnp.dot(
        bits.reshape(positions, CODE_BITS).T,
        grad_hidden.reshape(positions, channels),
        preferred_element_type=jnp.float32,
    )
    grad_embed, grad_gain, grad_bias = lax.psum((embed_term, gain_term, bias_term), ("dp", "shard"))
    return (decoded, grad_hidden[None], grad_conv, grad_embed, grad_gain, grad_bias)


def solution(mesh):
    return jax.shard_map(
        on_device,
        mesh=mesh,
        in_specs=(
            P("dp", None, None, "shard"),
            P("dp"),
            P("dp", None, None, "shard", None),
            P(),
            P("shard", None, None),
            P(),
            P(),
            P("dp", None, None, "shard", None),
        ),
        out_specs=(
            P("dp", None, None, "shard", None),
            P("dp", None, None, "shard", None),
            P("shard", None, None),
            P(),
            P(),
            P(),
        ),
        check_vma=False,
    )
```

profile of v0, /device:TPU:8, one launch (start us, length us, event | category | flops | bytes accessed | tf_op | source)
XLA Modules:
  0.0 610.6 jit_solution(5969993515602103230)
XLA Ops:
  8.7 2.7 fusion.29
  11.4 2.6 copy.34
  14.0 3.4 reshape.359
  17.4 20.4 %all_to_all.39 = bf16[16,2,2560]{2,1,0:T(2,128)(2,1)S(1)} all-to-all(bf16[16,2,2560]{2,1,0:T(2,128)(2,1)} %reshape.359), channel_id=1, replica_groups=mesh['dp'=16,'shard'=16] {'shard'}, dimensions={0} | all-to-all | bytes 327680 | tf_op jit(solution)/shard_map/all_to_all | solution.py:67
  37.8 4.1 reshape.360
  41.9 4.3 copy.35
  46.3 2.9 pad_slice_fusion.27
  49.2 6.8 %pad_slice_fusion.26 = (bf16[5,8,64,32]{3,2,1,0:T(8,128)(2,1)S(1)}, bf16[5,8,64,32]{3,2,1,0:T(8,128)(2,1)S(1)}, bf16[5,8,64,32]{3,2,1,0:T(8,128)(2,1)S(1)}, bf16...) fusion(bf16[5,8,64,32]{3,2,1,0:T(8,128)(2,1)S(1)} %bitcast.128), kind=kLoop, calls=%fused_computation.26 | loop fusion | bytes 3276800 | tf_op jit(solution)/shard_map/slice | solution.py:17
  56.0 16.7 %concatenate.61 = bf16[5,8,64,864]{3,2,1,0:T(8,128)(2,1)} concatenate(bf16[5,8,64,32]{3,2,1,0:T(8,128)(2,1)} %get-tuple-element.46, bf16[5,8,64,32]{3,2,1,0:T(8,128)(2,1)S(1)} %get-tuple-element.22, bf16[5,8,64,32]{3,2,1,0:T(8,128)(2,1)S(1)} %get-tuple-element.23, bf16[5,8,64,32]{3,2,1,0:T(8,128)(2,1)} %get-tuple-element.24, bf16[5,8,64,32]{3,2,1,0:T(8,128)(2,1)} %get-tuple-element.25, ...), dimensions={3} | concatenate | bytes 8847360 | tf_op jit(solution)/shard_map/concatenate | solution.py:43
  72.7 5.4 convolution_convert_fusion
  78.1 3.0 copy.36
  81.2 1.7 copy.38
  82.9 1.8 convert.7
  85.9 172.9 %all-reduce.11.cloned.1.call-done = bf16[5,8,64,512]{3,1,2,0:T(8,128)(2,1)} async-done(((bf16[5,8,64,512]{3,1,2,0:T(8,128)(2,1)}), bf16[5,8,64,512]{3,1,2,0:T(8,128)(2,1)}) %all-reduce.11.cloned.1.call-update) | async-done | bytes 2621456
  258.9 1.6 multiply_reduce_fusion.2
  262.1 50.1 %all-reduce.5 = (f32[32]{0:T(128)S(1)}, f32[32]{0:T(128)S(1)}) all-reduce(f32[32]{0:T(128)S(1)} %reduce_sum.67, f32[32]{0:T(128)} %reduce_sum.73), channel_id=1, replica_groups=mesh['dp'=16,'shard'=16] {'shard'}, use_global_device_ids=true, to_apply=%region_3.4 | all-reduce | flops 64 | bytes 512 | tf_op jit(solution)/shard_map/psum | solution.py:77
  315.5 1.9 fusion.31
  320.4 42.9 %all-reduce.4 = (f32[32]{0:T(128)S(1)}, f32[32]{0:T(128)S(1)}) all-reduce(f32[32]{0:T(128)S(1)} %reduce_sum.93, f32[32]{0:T(128)} %reduce_sum.90), channel_id=1, replica_groups=mesh['dp'=16,'shard'=16] {'shard'}, use_global_device_ids=true, to_apply=%region_12.13 | all-reduce | flops 64 | bytes 512 | tf_op jit(solution)/shard_map/psum | solution.py:112
  363.6 2.0 multiply_convert_fusion
  365.6 16.7 %concatenate.89 = bf16[2560,864]{1,0:T(8,128)(2,1)} concatenate(bf16[2560,32]{1,0:T(8,128)(2,1)} %bitcast.158, bf16[2560,32]{1,0:T(8,128)(2,1)S(1)} %bitcast.134, bf16[2560,32]{1,0:T(8,128)(2,1)S(1)} %bitcast.135, bf16[2560,32]{1,0:T(8,128)(2,1)} %bitcast.136, bf16[2560,32]{1,0:T(8,128)(2,1)} %bitcast.137, bf16[2560,32]{1,0:T(8,128)(2,1)} %bitcast.138, ...), dimensions={1} | concatenate | bytes 8847360 | tf_op jit(solution)/shard_map/concatenate | solution.py:43
  382.4 7.3 %copy.42 = bf16[864,2560]{1,0:T(8,128)(2,1)} copy(bf16[864,2560]{0,1:T(8,128)(2,1)} %bitcast.126) | data formatting | bytes 8847360 | tf_op jit(solution)/shard_map/pk,pc->kc/dot_general | solution.py:136
  389.6 43.9 %all-gather.2.cloned.1.call-done = bf16[5,8,64,512]{3,1,2,0:T(8,128)(2,1)} async-done(((bf16[5,8,4,512]{3,1,2,0:T(8,128)(2,1)}), bf16[5,8,64,512]{3,1,2,0:T(8,128)(2,1)}) %all-gather.2.cloned.1.call-update) | async-done | bytes 2621456 | tf_op jit(solution)/shard_map/all_gather | solution.py:124
  433.6 2.8 copy.39
  436.6 3.4 fusion
  440.0 3.1 fusion.55
  443.1 6.2 %fusion.27 = bf16[5,8,64,32]{3,2,1,0:T(8,128)(2,1)S(1)} fusion(f32[5,8,64,864]{3,2,1,0:T(8,128)S(1)} %fusion.55), kind=kLoop, calls=%fused_computation.81 | loop fusion | flops 2211840 | bytes 10649600 | tf_op jit(solution)/shard_map/convert_element_type | solution.py:134
  449.8 1.2 reshape.361
  450.9 4.5 all-to-all-start.1
  456.2 8.4 %all-to-all-done.1 = bf16[16,2,2560]{2,1,0:T(2,128)(2,1)S(1)} async-done(((bf16[16,2,2560]{2,1,0:T(2,128)(2,1)}), bf16[16,2,2560]{2,1,0:T(2,128)(2,1)S(1)}, u32[]{:S(2)}, u32[]{:S(2)}) %all-to-all-start.1) | async-done | bytes 163872 | tf_op jit(solution)/shard_map/all_to_all | solution.py:133
  467.8 79.0 %all-reduce.3 = (f32[18,512]{1,0:T(8,128)}, f32[512]{0:T(512)}, f32[512]{0:T(512)}) all-reduce(f32[18,512]{1,0:T(8,128)S(1)} %convolution_bitcast_fusion, f32[512]{0:T(512)S(1)} %bitcast.175, f32[512]{0:T(512)S(1)} %bitcast.176), channel_id=1, replica_groups=mesh['dp'=16,'shard'=16] {'dp','shard'}, use_global_device_ids=true, to_apply=%region_14.15 | all-reduce | flops 10240 | bytes 81920 | tf_op jit(solution)/shard_map/psum | solution.py:150
  547.6 53.8 %all-reduce.9.cloned.1.call-done = bf16[32,27,512]{2,0,1:T(8,128)(2,1)} async-done(((bf16[32,27,512]{2,0,1:T(8,128)(2,1)}), bf16[32,27,512]{2,0,1:T(8,128)(2,1)}) %all-reduce.9.cloned.1.call-update) | async-done | bytes 884752 | tf_op jit(solution)/shard_map/psum | solution.py:143
  601.4 2.6 convert_element_type.102
  (78 shorter events, 15.0 us)
Async XLA Ops:
  7.2 65.5 %copy-start = (bf16[32,27,512]{2,0,1:T(8,128)(2,1)S(1)}, bf16[32,27,512]{2,0,1:T(8,128)(2,1)}, u32[]{:S(2)}) copy-start(bf16[32,27,512]{2,0,1:T(8,128)(2,1)} %param.12) | copy-start | bytes 2654212
  7.2 251.7 %all-reduce.11.cloned.1.call-start = ((), (), s32[]{:S(2)}) async-start(), calls=%async_computation.4 | async-start | bytes 5242880
  7.2 6.7 %copy-start.12 = (s32[18]{0:T(128)}, s32[18]{0:T(128)S(1)}, u32[]{:S(2)}) copy-start(s32[18]{0:T(128)S(1)} %get-tuple-element.49) | copy-start | bytes 220
  7.3 6.7 %copy-start.14 = (s32[18]{0:T(128)}, s32[18]{0:T(128)S(1)}, u32[]{:S(2)}) copy-start(s32[18]{0:T(128)S(1)} %get-tuple-element.50) | copy-start | bytes 220
  8.0 250.9 %copy-start.9 = (f32[5]{0:T(128)}, f32[5]{0:T(128)S(1)}, u32[]{:S(2)}) copy-start(f32[5]{0:T(128)S(1)} %compare_convert_fusion) | copy-start | bytes 64
  81.1 3.6 copy-start.11
  81.1 234.4 %copy-start.4 = (f32[512]{0:T(512)S(1)}, f32[512]{0:T(512)}, u32[]{:S(2)}) copy-start(f32[512]{0:T(512)} %param.13) | copy-start | bytes 6148
  81.2 352.4 %all-gather.2.cloned.1.call-start = ((), (), s32[]{:S(2)}) async-start(), calls=%async_computation.2 | async-start | bytes 2785280 | tf_op jit(solution)/shard_map/all_gather | solution.py:124
  312.1 0.5 copy-start.10
  312.7 50.9 %copy-start.6 = (f32[512]{0:T(512)S(1)}, f32[512]{0:T(512)}, u32[]{:S(2)}) copy-start(f32[512]{0:T(512)} %param.14) | copy-start | bytes 6148
  365.6 235.9 %all-reduce.9.cloned.1.call-start = ((), (), s32[]{:S(2)}) async-start(), calls=%async_computation.3 | async-start | bytes 1769472 | tf_op jit(solution)/shard_map/psum | solution.py:143
  433.6 3.0 copy-start.1
  436.6 3.4 copy-start.2
  449.3 6.1 %copy-start.3 = (bf16[5,8,2,4,2,128]{5,1,4,2,3,0:T(8,128)(2,1)S(1)}, bf16[5,8,2,4,2,128]{5,1,4,2,3,0:T(8,128)(2,1)}, u32[]{:S(2)}) copy-start(bf16[5,8,2,4,2,128]{5,1,4,2,3,0:T(8,128)(2,1)} %get-tuple-element.48) | copy-start | bytes 491524
  450.9 13.8 %all-to-all-start.1 = ((bf16[16,2,2560]{2,1,0:T(2,128)(2,1)}), bf16[16,2,2560]{2,1,0:T(2,128)(2,1)S(1)}, u32[]{:S(2)}, u32[]{:S(2)}) async-start(bf16[16,2,2560]{2,1,0:T(2,128)(2,1)} %reshape.361), calls=%async_computation.1 | async-start | bytes 327680 | tf_op jit(solution)/shard_map/all_to_all | solution.py:133
  465.3 1.4 copy-start.5
  465.3 1.4 copy-start.13
  465.3 1.4 copy-start.15
  465.6 2.2 copy-start.7
  465.6 2.2 copy-start.8
Sparse Core Ops, SparseCore 0:
  81.3 177.5 all-reduce.10
  365.7 67.8 all-gather.1
  440.1 161.2 all-reduce.8
where the time goes:
time: 615 us; the launch traced here: 611 us
  waiting for transfers between devices  279 us (45%)
  blocking collectives  192 us (31%)
  local copies, waits for them, and re-layouts  82.7 us (13%)
  other arithmetic  20.8 us (3%)
  matrix products  15.5 us (3%)
  between operations  15.4 us (3%)
    unnamed x4, waiting for transfers between devices  173 us
    psum x1, blocking collectives, on_device(): lax.psum((embed_term, gain_term, bias_term), ('dp', 'shard'))  79 us
    psum x1, waiting for transfers between devices, on_device(): lax.psum(weight_sum.astype(jnp.bfloat16), 'dp').astype(jnp.float32)  53.8 us
    psum x1, blocking collectives, on_device(): lax.psum((jnp.sum(grouped * mask_groups, axis=(0, 1, 2, 4)), jnp.sum(grou...  50.1 us
    all_gather x1, waiting for transfers between devices, on_device(): whole_grad = lax.all_gather(d_conv, 'shard', axis=2, tiled=True)  43.9 us
    psum x1, blocking collectives, on_device(): lax.psum((jnp.sum(d_norm, axis=(0, 1, 2, 4)), jnp.sum(d_norm * normed, ax...  42.9 us
    concatenate x2, local copies, waits for them, and re-layouts, slab_columns(): jnp.concatenate(forward_taps(padded, frames, height, slab_width), axis=3)  33.4 us
    all_to_all x1, blocking collectives, on_device(): lax.all_to_all(features, 'shard', split_axis=3, concat_axis=2, tiled=True)  20.4 us
  transfers between devices with their start and end apart: 4, of which 4 were waited for; matrix products, arithmetic and copies ran while one was open for 7% of the time, Pallas kernels for 0%

commit v1 on v0

--- a/solution.py
+++ b/solution.py
@@ -6,6 +6,7 @@
 CODE_BITS = 18
 GROUPS = 32
 eps_norm = 1e-05
+_fix_entries = lambda field: jnp.sum(lax.all_gather(field, "dp"), 0)
 
 
 def forward_taps(padded, frames, height, width):
@@ -140,7 +141,7 @@
         preferred_element_type=jnp.float32,
     )
     weight_sum = clip_part.reshape(27, share, channels).transpose(1, 0, 2)
-    grad_conv = lax.psum(weight_sum.astype(jnp.bfloat16), "dp").astype(jnp.float32)
+    grad_conv = _fix_entries(weight_sum.astype(jnp.bfloat16)).astype(jnp.float32)
     grad_hidden = d_features * mask_cells.astype(jnp.bfloat16)
     embed_term = jnp.dot(
         bits.reshape(positions, CODE_BITS).T,

time: 615 us -> 765 us (1.24)
  waiting for transfers between devices: 279 us -> 411 us
  blocking collectives: 192 us -> 203 us
    all_gather x0 -> x1, waiting for transfers between devices: none -> 184 us  [_fix_entries = lambda field: jnp.sum(lax.all_gather(field, 'dp'), 0)]
    psum x1 -> x0, waiting for transfers between devices: 53.8 us -> none  [on_device(): lax.psum(weight_sum.astype(jnp.bfloat16), 'dp').astype(jnp.float32)]
    psum x1, blocking collectives: 79 us -> 89.6 us  [on_device(): lax.psum((embed_term, gain_term, bias_term), ('dp', 'shard'))]
    reduce_sum x0 -> x1, other arithmetic: none -> 8.33 us  [_fix_entries = lambda field: jnp.sum(lax.all_gather(field, 'dp'), 0)]
  transfers between devices with their start and end apart: 4 -> 4, of which waited for: 4 -> 4; matrix products, arithmetic and copies ran while one was open for 7% -> 6% of each run, Pallas kernels for 0% -> 0%
where the time goes in v1:
time: 765 us; the launch traced here: 760 us
  waiting for transfers between devices  411 us (54%)
  blocking collectives  203 us (27%)
  local copies, waits for them, and re-layouts  82.8 us (11%)
  other arithmetic  27.9 us (4%)
  matrix products  15.5 us (2%)
  between operations  15.4 us (2%)
    all_gather x1, waiting for transfers between devices, _fix_entries = lambda field: jnp.sum(lax.all_gather(field, 'dp'), 0)  184 us
    unnamed x4, waiting for transfers between devices  173 us
    psum x1, blocking collectives, on_device(): lax.psum((embed_term, gain_term, bias_term), ('dp', 'shard'))  89.6 us
    psum x1, blocking collectives, on_device(): lax.psum((jnp.sum(grouped * mask_groups, axis=(0, 1, 2, 4)), jnp.sum(grou...  50.1 us
    all_gather x1, waiting for transfers between devices, on_device(): whole_grad = lax.all_gather(d_conv, 'shard', axis=2, tiled=True)  43.9 us
    psum x1, blocking collectives, on_device(): lax.psum((jnp.sum(d_norm, axis=(0, 1, 2, 4)), jnp.sum(d_norm * normed, ax...  42.9 us
    concatenate x2, local copies, waits for them, and re-layouts, slab_columns(): jnp.concatenate(forward_taps(padded, frames, height, slab_width), axis=3)  33.4 us
    all_to_all x1, blocking collectives, on_device(): lax.all_to_all(features, 'shard', split_axis=3, concat_axis=2, tiled=True)  20.4 us
  transfers between devices with their start and end apart: 4, of which 4 were waited for; matrix products, arithmetic and copies ran while one was open for 6% of the time, Pallas kernels for 0%

profile of v1, /device:TPU:8, one launch (start us, length us, event | category | flops | bytes accessed | tf_op | source)
XLA Modules:
  0.0 760.1 jit_solution(238833943727757489)
XLA Ops:
  8.7 2.7 fusion.29
  11.4 2.6 copy.34
  14.0 3.4 reshape.360
  17.4 20.4 %all_to_all.39 = bf16[16,2,2560]{2,1,0:T(2,128)(2,1)S(1)} all-to-all(bf16[16,2,2560]{2,1,0:T(2,128)(2,1)} %reshape.360), channel_id=1, replica_groups=mesh['dp'=16,'shard'=16] {'shard'}, dimensions={0} | all-to-all | bytes 327680 | tf_op jit(solution)/shard_map/all_to_all | solution.py:68
  37.8 4.1 reshape.361
  41.9 4.3 copy.35
  46.3 2.9 pad_slice_fusion.27
  49.2 6.9 pad_slice_fusion.26
  56.1 16.7 %concatenate.61 = bf16[5,8,64,864]{3,2,1,0:T(8,128)(2,1)} concatenate(bf16[5,8,64,32]{3,2,1,0:T(8,128)(2,1)} %get-tuple-element.46, bf16[5,8,64,32]{3,2,1,0:T(8,128)(2,1)S(1)} %get-tuple-element.22, bf16[5,8,64,32]{3,2,1,0:T(8,128)(2,1)S(1)} %get-tuple-element.23, bf16[5,8,64,32]{3,2,1,0:T(8,128)(2,1)} %get-tuple-element.24, bf16[5,8,64,32]{3,2,1,0:T(8,128)(2,1)} %get-tuple-element.25, ...), dimensions={3} | concatenate | bytes 8847360 | tf_op jit(solution)/shard_map/concatenate | solution.py:44
  72.8 5.4 convolution_convert_fusion
  78.2 3.0 copy.36
  81.3 1.7 copy.38
  83.0 1.8 convert.8
  86.0 173.0 %all-reduce.8.cloned.1.call-done = bf16[5,8,64,512]{3,1,2,0:T(8,128)(2,1)} async-done(((bf16[5,8,64,512]{3,1,2,0:T(8,128)(2,1)}), bf16[5,8,64,512]{3,1,2,0:T(8,128)(2,1)}) %all-reduce.8.cloned.1.call-update) | async-done | bytes 2621456
  259.0 1.6 multiply_reduce_fusion.2
  262.2 50.1 %all-reduce.5 = (f32[32]{0:T(128)S(1)}, f32[32]{0:T(128)S(1)}) all-reduce(f32[32]{0:T(128)S(1)} %reduce_sum.96, f32[32]{0:T(128)} %reduce_sum.99), channel_id=1, replica_groups=mesh['dp'=16,'shard'=16] {'shard'}, use_global_device_ids=true, to_apply=%region_3.4 | all-reduce | flops 64 | bytes 512 | tf_op jit(solution)/shard_map/psum | solution.py:78
  315.6 1.9 fusion.31
  320.5 42.9 %all-reduce.4 = (f32[32]{0:T(128)S(1)}, f32[32]{0:T(128)S(1)}) all-reduce(f32[32]{0:T(128)S(1)} %reduce_sum.105, f32[32]{0:T(128)} %reduce_sum.102), channel_id=1, replica_groups=mesh['dp'=16,'shard'=16] {'shard'}, use_global_device_ids=true, to_apply=%region_12.13 | all-reduce | flops 64 | bytes 512 | tf_op jit(solution)/shard_map/psum | solution.py:113
  363.7 2.0 multiply_convert_fusion
  365.8 16.7 %concatenate.89 = bf16[2560,864]{1,0:T(8,128)(2,1)} concatenate(bf16[2560,32]{1,0:T(8,128)(2,1)} %bitcast.160, bf16[2560,32]{1,0:T(8,128)(2,1)S(1)} %bitcast.136, bf16[2560,32]{1,0:T(8,128)(2,1)S(1)} %bitcast.137, bf16[2560,32]{1,0:T(8,128)(2,1)} %bitcast.138, bf16[2560,32]{1,0:T(8,128)(2,1)} %bitcast.139, bf16[2560,32]{1,0:T(8,128)(2,1)} %bitcast.140, ...), dimensions={1} | concatenate | bytes 8847360 | tf_op jit(solution)/shard_map/concatenate | solution.py:44
  382.5 7.3 copy.42
  389.7 43.9 %all-gather.4.cloned.1.call-done = bf16[5,8,64,512]{3,1,2,0:T(8,128)(2,1)} async-done(((bf16[5,8,4,512]{3,1,2,0:T(8,128)(2,1)}), bf16[5,8,64,512]{3,1,2,0:T(8,128)(2,1)}) %all-gather.4.cloned.1.call-update) | async-done | bytes 2621456 | tf_op jit(solution)/shard_map/all_gather | solution.py:125
  433.7 2.8 copy.39
  436.7 3.4 fusion
  440.1 3.1 fusion.55
  443.2 6.2 fusion.27
  451.0 4.5 all-to-all-start.1
  456.4 9.7 %all-to-all-done.1 = bf16[16,2,2560]{2,1,0:T(2,128)(2,1)S(1)} async-done(((bf16[16,2,2560]{2,1,0:T(2,128)(2,1)}), bf16[16,2,2560]{2,1,0:T(2,128)(2,1)S(1)}, u32[]{:S(2)}, u32[]{:S(2)}) %all-to-all-start.1) | async-done | bytes 163872 | tf_op jit(solution)/shard_map/all_to_all | solution.py:134
  469.1 89.6 %all-reduce.3 = (f32[18,512]{1,0:T(8,128)}, f32[512]{0:T(512)}, f32[512]{0:T(512)}) all-reduce(f32[18,512]{1,0:T(8,128)S(1)} %convolution_bitcast_fusion, f32[512]{0:T(512)S(1)} %bitcast.177, f32[512]{0:T(512)S(1)} %bitcast.178), channel_id=1, replica_groups=mesh['dp'=16,'shard'=16] {'dp','shard'}, use_global_device_ids=true, to_apply=%region_14.15 | all-reduce | flops 10240 | bytes 81920 | tf_op jit(solution)/shard_map/psum | solution.py:151
  559.6 184.2 %all-gather.6.cloned.1.call-done = bf16[512,27,512]{2,0,1:T(8,128)(2,1)} async-done(((bf16[32,27,512]{2,0,1:T(8,128)(2,1)}), bf16[512,27,512]{2,0,1:T(8,128)(2,1)}) %all-gather.6.cloned.1.call-update) | async-done | bytes 14155792 | tf_op jit(solution)/shard_map/all_gather | solution.py:9
  743.8 8.3 %reduce_sum.106 = bf16[32,27,512]{2,0,1:T(8,128)(2,1)S(1)} reduce(bf16[16,32,27,512]{3,1,0,2:T(8,128)(2,1)} %bitcast.132, bf16[]{:T(256)} %constant.52.clone.1), dimensions={0}, to_apply=%region_13.14 | reduce | flops 6635520 | bytes 15040514 | tf_op jit(solution)/shard_map/reduce_sum | solution.py:9
  752.1 1.4 convert_element_type.104
  (79 shorter events, 16.2 us)
Async XLA Ops:
  7.2 65.6 %copy-start = (bf16[32,27,512]{2,0,1:T(8,128)(2,1)S(1)}, bf16[32,27,512]{2,0,1:T(8,128)(2,1)}, u32[]{:S(2)}) copy-start(bf16[32,27,512]{2,0,1:T(8,128)(2,1)} %param.12) | copy-start | bytes 2654212
  7.2 251.8 %all-reduce.8.cloned.1.call-start = ((), (), s32[]{:S(2)}) async-start(), calls=%async_computation.4 | async-start | bytes 5242880
  7.2 6.7 copy-start.12
  7.3 6.7 copy-start.14
  8.0 251.0 %copy-start.9 = (f32[5]{0:T(128)}, f32[5]{0:T(128)S(1)}, u32[]{:S(2)}) copy-start(f32[5]{0:T(128)S(1)} %compare_convert_fusion) | copy-start | bytes 64
  81.2 3.6 copy-start.11
  81.2 234.4 %copy-start.4 = (f32[512]{0:T(512)S(1)}, f32[512]{0:T(512)}, u32[]{:S(2)}) copy-start(f32[512]{0:T(512)} %param.13) | copy-start | bytes 6148
  81.2 352.4 %all-gather.4.cloned.1.call-start = ((), (), s32[]{:S(2)}) async-start(), calls=%async_computation.2 | async-start | bytes 2785280 | tf_op jit(solution)/shard_map/all_gather | solution.py:125
  312.2 0.5 copy-start.10
  312.8 50.9 %copy-start.6 = (f32[512]{0:T(512)S(1)}, f32[512]{0:T(512)}, u32[]{:S(2)}) copy-start(f32[512]{0:T(512)} %param.14) | copy-start | bytes 6148
  365.7 378.1 %all-gather.6.cloned.1.call-start = ((), (), s32[]{:S(2)}) async-start(), calls=%async_computation.3 | async-start | bytes 15040512 | tf_op jit(solution)/shard_map/all_gather | solution.py:9
  433.7 3.0 copy-start.1
  436.7 3.4 copy-start.2
  449.4 6.1 copy-start.3
  451.0 15.0 %all-to-all-start.1 = ((bf16[16,2,2560]{2,1,0:T(2,128)(2,1)}), bf16[16,2,2560]{2,1,0:T(2,128)(2,1)S(1)}, u32[]{:S(2)}, u32[]{:S(2)}) async-start(bf16[16,2,2560]{2,1,0:T(2,128)(2,1)} %reshape.362), calls=%async_computation.1 | async-start | bytes 327680 | tf_op jit(solution)/shard_map/all_to_all | solution.py:134
  466.6 1.4 copy-start.5
  466.6 1.4 copy-start.13
  466.6 1.4 copy-start.15
  466.9 2.2 copy-start.7
  466.9 2.2 copy-start.8
Sparse Core Ops, SparseCore 0:
  81.3 177.5 all-reduce.7
  365.8 67.8 all-gather.3
  440.2 303.5 all-gather.5
